TPU v7x, 32 devices: a whole 2x2x4 slice. The times are simulated.
32 devices in a mesh: band: 4 (over y, x), region: 8 (over z, core).
Axes of the slice: x: 2, y: 2, z: 4, core: 2. Of those that a mesh axis runs over, the one named last changes fastest.
Arguments:
- fields: float32 [8192, 512], P(('band', 'region')), may hold values from -6 to 6
- send_list: int32 [4, 8, 4, 2], replicated, may hold values from -1 to 1, as said below
- departure: int32 [16, 8192], P(None, ('band', 'region')), may hold values from 0 to 1279, as said below
- hweight: float32 [16, 8192], P(None, ('band', 'region')), may hold values from -0.2 to 0.5
- base_level: int32 [128, 8192], P(None, ('band', 'region')), may hold values from 1 to 125
- vweight: float32 [4, 128, 8192], P(None, None, ('band', 'region')), may hold values from -0.25 to 0.75
- vertical_op: float32 [128, 128], replicated, may hold values from -0.4 to 2, as said below
Outputs:
- level_shards: float32 [512, 8192], P('region', 'band')
Inputs may be any that keep to these rules, and one draw needn't show every extreme that they name: send_list[b, r, d] names distinct block numbers of device (b, r), each block being 128 consecutive points of it; a list holds 1 to 2 numbers followed by -1 in the remaining entries, and in every draw some region's lists are all full. departure[c, p] indexes the extended rows of point p's device: below 256 the device's own point, else 256 + d * 2 * 128 + s for row s of part d; only rows delivered by an existing neighbour from a list entry that is not -1 are named. vertical_op[k, l] is zero where k and l differ by more than 2.
All inputs are finite; a program needn't handle non-finite values.
Results may differ from a plain program's by a relative error of at most 0.0003.
Values sent between devices are 32-bit elements; how exact they have to be, the bound alone decides.
No kernel may reach another device: no remote copies, remote signals or barrier semaphores. Data moves between devices by JAX's collectives and lax.ppermute only.
A program may use at most 64 MiB of HBM per device.

v0:
```python
import jax
import jax.numpy as jnp
from jax import lax
from jax.sharding import PartitionSpec as P

BLK = 128
exact_mode = lax.Precision.HIGHEST


def from_behind(block, axis, distance):
    devices = range(lax.axis_size(axis))
    route = [(i - distance, i) for i in devices if i - distance in devices]
    return lax.ppermute(block, axis, route)


def from_behind_2(block, axis, distance):
    devices = range(lax.axis_size(axis))
    route = [((i - distance) % len(devices), i) for i in devices]
    return lax.ppermute(block, axis, route)


def padded_2(x, sides, width):
    for axis, dim in sides:
        size, length = (lax.axis_size(axis), x.shape[dim])
        up = [(i, (i + 1) % size) for i in range(size - 1)]
        down = [(j, i) for i, j in up]
        last = lax.slice_in_dim(x, length - width, length, axis=dim)
        initial = lax.slice_in_dim(x, 0, width, axis=dim)
        before = lax.ppermute(last, axis, up)
        after = lax.ppermute(initial, axis, down)
        x = jnp.concatenate([before, x, after], axis=dim)
    return x


def pack_blocks(block_table, block_list):
    safe_list = jnp.maximum(block_list, 0)
    picked = jnp.take(block_table, safe_list, axis=0)
    keeping = (block_list >= 0)[:, None, None]
    picked = jnp.where(keeping, picked, jnp.zeros((), picked.dtype))
    return picked.reshape(-1, picked.shape[-1])


def column_update(extended, depart_block, hweight_block, base_block, vweight_block, vertical_op):
    stencil_len, point_count = depart_block.shape
    width_all = extended.shape[1]
    levels = vertical_op.shape[0]
    fields_count = width_all // levels
    picked = jnp.take(extended, depart_block.reshape(-1), axis=0).reshape(
        stencil_len, point_count, width_all
    )
    horizontal = jnp.sum(hweight_block[:, :, None] * picked, axis=0)
    stacked = jnp.transpose(horizontal).reshape(fields_count, levels, point_count)
    source_ids = jnp.arange(levels, dtype=jnp.int32)[None, :, None]
    level_weights = jnp.zeros((levels, levels, point_count), jnp.float32)
    for offset in range(4):
        target = (base_block + (offset - 1))[:, None, :]
        level_weights = level_weights + jnp.where(
            target == source_ids, vweight_block[offset][:, None, :], jnp.zeros((), jnp.float32)
        )
    interpolated = jnp.einsum("klp,flp->fkp", level_weights, stacked, precision=exact_mode)
    return interpolated.reshape(width_all, point_count)


def body(fields, send_list, departure, hweight, base_level, vweight, vertical_op):
    point_total, width_all = fields.shape
    levels = vertical_op.shape[0]
    block_table = fields.reshape(point_total // BLK, BLK, width_all)
    band_id = lax.axis_index("band")
    region_id = lax.axis_index("region")
    region_count = lax.axis_size("region")
    own_lists = send_list[band_id, region_id]
    from_north = from_behind(pack_blocks(block_table, own_lists[0]), "band", 1)
    from_south = from_behind(pack_blocks(block_table, own_lists[1]), "band", -1)
    from_west = from_behind_2(pack_blocks(block_table, own_lists[2]), "region", 1)
    from_east = from_behind_2(pack_blocks(block_table, own_lists[3]), "region", -1)
    extended = jnp.concatenate([fields, from_north, from_south, from_west, from_east], axis=0)
    step_points = min(128, point_total)

    def one_step(step_id, result):
        first_col = step_id * step_points
        updated = column_update(
            extended,
            lax.dynamic_slice_in_dim(departure, first_col, step_points, 1),
            lax.dynamic_slice_in_dim(hweight, first_col, step_points, 1),
            lax.dynamic_slice_in_dim(base_level, first_col, step_points, 1),
            lax.dynamic_slice_in_dim(vweight, first_col, step_points, 2),
            vertical_op,
        )
        return lax.dynamic_update_slice_in_dim(result, updated, first_col, 1)

    result = lax.fori_loop(
        0, point_total // step_points, one_step, jnp.zeros((width_all, point_total), jnp.float32)
    )
    shard_rows = lax.all_to_all(result, "region", split_axis=0, concat_axis=1, tiled=True)
    row_count = width_all // region_count
    padded = padded_2(shard_rows, (("region", 0),), 2)
    global_rows = region_id * row_count + jnp.arange(row_count, dtype=jnp.int32)
    level_ids = global_rows % levels
    operated = jnp.zeros(shard_rows.shape, jnp.float32)
    for offset in range(-2, 3):
        target = level_ids + offset
        valid = (target >= 0) & (target < levels)
        coeff = vertical_op[level_ids, jnp.clip(target, 0, levels - 1)]
        coeff = jnp.where(valid, coeff, jnp.zeros((), jnp.float32))
        operated = operated + coeff[:, None] * padded[2 + offset : 2 + offset + row_count, :]
    return operated


def solution(mesh):
    placed = (
        P(("band", "region"), None),
        P(),
        P(None, ("band", "region")),
        P(None, ("band", "region")),
        P(None, ("band", "region")),
        P(None, None, ("band", "region")),
        P(),
    )
    return jax.shard_map(
        body, mesh=mesh, in_specs=placed, out_specs=P("region", "band"), check_vma=False
    )
```

profile of v0, /device:TPU:1, one launch (start us, length us, event | category | flops | bytes accessed | tf_op | source)
XLA Modules:
  0.0 178.1 jit_solution(16740423676924799088)
XLA Ops:
  0.0 1.0 maximum_reduce_fusion
  1.0 1.0 compare_reduce_fusion
  2.0 1.6 gather_fusion.6
  3.6 0.9 select_select_fusion.3
  4.6 4.7 %collective-permute-start = (f32[256,512]{1,0:T(8,128)}, f32[256,512]{1,0:T(8,128)}, u32[]{:S(2)}, u32[]{:S(2)}) collective-permute-start(f32[256,512]{1,0:T(8,128)} %bitcast.11), channel_id=1, source_target_pairs={{0,8},{8,16},{16,24},{1,9},{9,17},{17,25},{2,10},{10,18},{18,26},{... | collective-permute-start | bytes 1572872 | tf_op jit(solution)/shard_map/ppermute | solution.py:13
  9.3 1.6 gather_fusion.7
  10.9 0.9 select_select_fusion.2
  11.9 1.3 collective-permute-start.1
  13.2 0.6 gather_fusion.8
  13.8 0.9 select_select_fusion.1
  14.8 2.1 %collective-permute-start.2 = (f32[256,512]{1,0:T(8,128)}, f32[256,512]{1,0:T(8,128)}, u32[]{:S(2)}, u32[]{:S(2)}) collective-permute-start(f32[256,512]{1,0:T(8,128)} %bitcast.13), channel_id=1, source_target_pairs={{7,0},{0,1},{1,2},{2,3},{3,4},{4,5},{5,6},{6,7},{15,8},{8,9},{9,10... | collective-permute-start | bytes 1572872 | tf_op jit(solution)/shard_map/ppermute | solution.py:19
  16.9 0.6 gather_fusion.9
  17.5 0.9 select_select_fusion
  18.4 0.0 collective-permute-start.3
  18.5 0.9 collective-permute-done
  19.4 1.1 constant_dynamic-update-slice_fusion.4
  20.5 12.1 %collective-permute-done.1 = f32[256,512]{1,0:T(8,128)} collective-permute-done((f32[256,512]{1,0:T(8,128)}, f32[256,512]{1,0:T(8,128)}, u32[]{:S(2)}, u32[]{:S(2)}) %collective-permute-start.1) | collective-permute-done | bytes 524320 | tf_op jit(solution)/shard_map/ppermute | solution.py:13
  32.6 1.1 constant_dynamic-update-slice_fusion.3
  33.7 0.0 collective-permute-done.2
  33.7 1.1 constant_dynamic-update-slice_fusion.2
  34.8 1.1 constant_dynamic-update-slice_fusion.1
  35.9 0.8 broadcast_in_dim.186.clone
  36.7 112.9 %while.13 = (s32[]{:T(128)}, f32[512,256]{1,0:T(8,128)}, f32[16,256]{1,0:T(8,128)}, s32[16,256]{1,0:T(8,128)}, f32[1280,512]{1,0:T(8,128)S(1)}, /*index=5*/s32[1...) while((s32[]{:T(128)}, f32[512,256]{1,0:T(8,128)}, ...), condition=%wide.region_2.4_spmd, body=%wide.region_0.3_spmd.sunk | while | flops 126881800 | bytes 17125624 | solution.py:91
  36.7 0.7 compare_and_fusion.6
  37.4 8.9 %gather_fusion = f32[2048,512]{1,0:T(8,128)} fusion(f32[1280,512]{1,0:T(8,128)S(1)} %get-tuple-element.290, s32[2048]{0:T(1024)S(1)} %broadcast_clamp_fusion.2), kind=kCustom, calls=%fused_computation.1.clone.1 | custom fusion | bytes 8396800 | tf_op jit(solution)/shard_map/while/body/eval_jaxpr/jit(_take)/gather | solution.py:48
  46.3 0.7 constant_dynamic-slice_fusion.15
  47.0 2.6 %multiply_reduce_fusion.2 = f32[128,512]{1,0:T(8,128)S(1)} fusion(f32[16,128,512]{2,1,0:T(8,128)} %bitcast.59, f32[16,128]{1,0:T(8,128)S(1)} %constant_dynamic-slice_fusion.15, pred[16,128]{1,0:T(8,128)(4,1)S(1)} %get-tuple-element.250), kind=kLoop, calls=%fused_computation.31.clone.1 | loop fusion | flops 3080192 | bytes 4466688 | tf_op jit(solution)/shard_map/while/body/eval_jaxpr/reduce_sum | solution.py:51
  49.6 0.1 reshape.413
  49.7 1.0 constant_dynamic-slice_fusion.16
  50.7 0.1 copy.34
  50.8 0.1 copy.36
  50.9 0.1 copy.37
  51.0 0.1 copy.38
  51.1 0.9 constant_dynamic-slice_fusion.17
  51.9 0.1 copy.35
  52.1 40.2 %fusion.62 = f32[4,128,128]{1,0,2:T(4,128)S(1)} fusion(f32[4,128,128]{1,0,2:T(4,128)S(1)} %reshape.413, f32[128,128]{0,1:T(8,128)S(1)} %bitcast.71, s32[128,128]{0,1:T(8,128)S(1)} %get-tuple-element.252, f32[128,128]{0,1:T(8,128)S(1)} %bitcast.72, s32[128,128]{0,1:T(8,128)S(1)} %get-tuple-element.254, f32[128,128]{0,1:T(8,128)S(1)} %bitcast.73, ...), kind=kOutput, calls=%fused_computation.32.clone.2 | convolution fusion | flops 123731968 | bytes 1048576 | tf_op jit(solution)/shard_map/while/body/eval_jaxpr/klp,flp->fkp/dot_general | solution.py:60
  92.2 0.1 copy.39
  92.4 0.7 constant_dynamic-update-slice_fusion.9
  93.1 0.7 compare_and_fusion.6
  93.9 8.9 %gather_fusion = f32[2048,512]{1,0:T(8,128)} fusion(f32[1280,512]{1,0:T(8,128)S(1)} %get-tuple-element.290, s32[2048]{0:T(1024)S(1)} %broadcast_clamp_fusion.2), kind=kCustom, calls=%fused_computation.1.clone.1 | custom fusion | bytes 8396800 | tf_op jit(solution)/shard_map/while/body/eval_jaxpr/jit(_take)/gather | solution.py:48
  102.8 0.7 constant_dynamic-slice_fusion.15
  103.5 2.6 %multiply_reduce_fusion.2 = f32[128,512]{1,0:T(8,128)S(1)} fusion(f32[16,128,512]{2,1,0:T(8,128)} %bitcast.59, f32[16,128]{1,0:T(8,128)S(1)} %constant_dynamic-slice_fusion.15, pred[16,128]{1,0:T(8,128)(4,1)S(1)} %get-tuple-element.250), kind=kLoop, calls=%fused_computation.31.clone.1 | loop fusion | flops 3080192 | bytes 4466688 | tf_op jit(solution)/shard_map/while/body/eval_jaxpr/reduce_sum | solution.py:51
  106.1 0.1 reshape.413
  106.2 1.0 constant_dynamic-slice_fusion.16
  107.1 0.1 copy.34
  107.2 0.1 copy.36
  107.3 0.1 copy.37
  107.4 0.1 copy.38
  107.5 0.9 constant_dynamic-slice_fusion.17
  108.4 0.1 copy.35
  108.5 40.2 %fusion.62 = f32[4,128,128]{1,0,2:T(4,128)S(1)} fusion(f32[4,128,128]{1,0,2:T(4,128)S(1)} %reshape.413, f32[128,128]{0,1:T(8,128)S(1)} %bitcast.71, s32[128,128]{0,1:T(8,128)S(1)} %get-tuple-element.252, f32[128,128]{0,1:T(8,128)S(1)} %bitcast.72, s32[128,128]{0,1:T(8,128)S(1)} %get-tuple-element.254, f32[128,128]{0,1:T(8,128)S(1)} %bitcast.73, ...), kind=kOutput, calls=%fused_computation.32.clone.2 | convolution fusion | flops 123731968 | bytes 1048576 | tf_op jit(solution)/shard_map/while/body/eval_jaxpr/klp,flp->fkp/dot_general | solution.py:60
  148.7 0.1 copy.39
  148.9 0.7 constant_dynamic-update-slice_fusion.9
  149.6 6.4 %all-to-all-start = ((f32[8,64,256]{2,1,0:T(8,128)}), f32[8,64,256]{2,1,0:T(8,128)S(1)}, u32[]{:S(2)}, u32[]{:S(2)}) async-start(f32[8,64,256]{2,1,0:T(8,128)} %bitcast.70), calls=%async_computation | async-start | bytes 1048576 | tf_op jit(solution)/shard_map/all_to_all | solution.py:94
  156.0 0.8 gather_fusion.4
  156.8 0.8 gather_fusion.5
  157.6 0.8 gather_fusion.2
  158.4 0.8 gather_fusion.3
  159.2 0.8 gather_fusion.1
  160.1 10.3 %all-to-all-done = f32[8,64,256]{2,1,0:T(8,128)S(1)} async-done(((f32[8,64,256]{2,1,0:T(8,128)}), f32[8,64,256]{2,1,0:T(8,128)S(1)}, u32[]{:S(2)}, u32[]{:S(2)}) %all-to-all-start) | async-done | bytes 524320 | tf_op jit(solution)/shard_map/all_to_all | solution.py:94
  170.4 2.9 %collective-permute-start.5 = (f32[2,2048]{1,0:T(2,128)S(1)}, f32[2,2048]{1,0:T(2,128)S(1)}, u32[]{:S(2)}, u32[]{:S(2)}) collective-permute-start(f32[2,2048]{1,0:T(2,128)S(1)} %bitcast.78), channel_id=1, source_target_pairs={{1,0},{2,1},{3,2},{4,3},{5,4},{6,5},{7,6},{9,8},{10,9},{11,10},{12... | collective-permute-start | bytes 49160 | tf_op jit(solution)/shard_map/ppermute | solution.py:30
  173.3 2.7 %collective-permute-start.4 = (f32[2,2048]{1,0:T(2,128)S(1)}, f32[2,2048]{1,0:T(2,128)S(1)}, u32[]{:S(2)}, u32[]{:S(2)}) collective-permute-start(f32[2,2048]{1,0:T(2,128)S(1)} %bitcast.77), channel_id=1, source_target_pairs={{0,1},{1,2},{2,3},{3,4},{4,5},{5,6},{6,7},{8,9},{9,10},{10,11},{11... | collective-permute-start | bytes 49160 | tf_op jit(solution)/shard_map/ppermute | solution.py:29
  176.1 0.8 collective-permute-done.4
  176.9 1.2 fusion.26
  (33 shorter events, 0.4 us)
Async XLA Ops:
  0.0 156.0 %copy-start = (f32[128,128]{1,0:T(8,128)S(1)}, f32[128,128]{1,0:T(8,128)}, u32[]{:S(2)}) copy-start(f32[128,128]{1,0:T(8,128)} %param.17) | copy-start | bytes 196612
  0.0 13.2 %copy-start.1 = (f32[256,512]{1,0:T(8,128)S(1)}, f32[256,512]{1,0:T(8,128)}, u32[]{:S(2)}) copy-start(f32[256,512]{1,0:T(8,128)} %param.11) | copy-start | bytes 1572868
  4.6 14.8 %collective-permute-start = (f32[256,512]{1,0:T(8,128)}, f32[256,512]{1,0:T(8,128)}, u32[]{:S(2)}, u32[]{:S(2)}) collective-permute-start(f32[256,512]{1,0:T(8,128)} %bitcast.11), channel_id=1, source_target_pairs={{0,8},{8,16},{16,24},{1,9},{9,17},{17,25},{2,10},{10,18},{18,26},{... | collective-permute-start | bytes 1572872 | tf_op jit(solution)/shard_map/ppermute | solution.py:13
  11.9 20.7 %collective-permute-start.1 = (f32[256,512]{1,0:T(8,128)}, f32[256,512]{1,0:T(8,128)}, u32[]{:S(2)}, u32[]{:S(2)}) collective-permute-start(f32[256,512]{1,0:T(8,128)} %bitcast.12), channel_id=1, source_target_pairs={{8,0},{16,8},{24,16},{9,1},{17,9},{25,17},{10,2},{18,10},{26,18},{... | collective-permute-start | bytes 1572872 | tf_op jit(solution)/shard_map/ppermute | solution.py:13
  14.8 18.9 %collective-permute-start.2 = (f32[256,512]{1,0:T(8,128)}, f32[256,512]{1,0:T(8,128)}, u32[]{:S(2)}, u32[]{:S(2)}) collective-permute-start(f32[256,512]{1,0:T(8,128)} %bitcast.13), channel_id=1, source_target_pairs={{7,0},{0,1},{1,2},{2,3},{3,4},{4,5},{5,6},{6,7},{15,8},{8,9},{9,10... | collective-permute-start | bytes 1572872 | tf_op jit(solution)/shard_map/ppermute | solution.py:19
  18.4 16.3 %collective-permute-start.3 = (f32[256,512]{1,0:T(8,128)}, f32[256,512]{1,0:T(8,128)}, u32[]{:S(2)}, u32[]{:S(2)}) collective-permute-start(f32[256,512]{1,0:T(8,128)} %bitcast.14), channel_id=1, source_target_pairs={{1,0},{2,1},{3,2},{4,3},{5,4},{6,5},{7,6},{0,7},{9,8},{10,9},{11,1... | collective-permute-start | bytes 1572872 | tf_op jit(solution)/shard_map/ppermute | solution.py:19
  149.6 20.8 %all-to-all-start = ((f32[8,64,256]{2,1,0:T(8,128)}), f32[8,64,256]{2,1,0:T(8,128)S(1)}, u32[]{:S(2)}, u32[]{:S(2)}) async-start(f32[8,64,256]{2,1,0:T(8,128)} %bitcast.70), calls=%async_computation | async-start | bytes 1048576 | tf_op jit(solution)/shard_map/all_to_all | solution.py:94
  170.4 5.6 %collective-permute-start.5 = (f32[2,2048]{1,0:T(2,128)S(1)}, f32[2,2048]{1,0:T(2,128)S(1)}, u32[]{:S(2)}, u32[]{:S(2)}) collective-permute-start(f32[2,2048]{1,0:T(2,128)S(1)} %bitcast.78), channel_id=1, source_target_pairs={{1,0},{2,1},{3,2},{4,3},{5,4},{6,5},{7,6},{9,8},{10,9},{11,10},{12... | collective-permute-start | bytes 49160 | tf_op jit(solution)/shard_map/ppermute | solution.py:30
  173.3 3.5 %collective-permute-start.4 = (f32[2,2048]{1,0:T(2,128)S(1)}, f32[2,2048]{1,0:T(2,128)S(1)}, u32[]{:S(2)}, u32[]{:S(2)}) collective-permute-start(f32[2,2048]{1,0:T(2,128)S(1)} %bitcast.77), channel_id=1, source_target_pairs={{0,1},{1,2},{2,3},{3,4},{4,5},{5,6},{6,7},{8,9},{9,10},{10,11},{11... | collective-permute-start | bytes 49160 | tf_op jit(solution)/shard_map/ppermute | solution.py:29
where the time goes:
time: 179 us; the launch traced here: 178 us
  matrix products  80.4 us (45%)
  local copies, waits for them, and re-layouts  39.3 us (22%)
  waiting for transfers between devices  24.1 us (13%)
  starting transfers between devices  20.1 us (11%)
  other arithmetic  13.8 us (8%)
    dot_general x2, matrix products, column_update(): jnp.einsum('klp,flp->fkp', level_weights, stacked, precision=exact_mode)  80.4 us
    gather x2, local copies, waits for them, and re-layouts, column_update(): jnp.take(extended, depart_block.reshape(-1), axis=0)  17.8 us
    ppermute x2, waiting for transfers between devices, from_behind(): return lax.ppermute(block, axis, route)  13 us
    all_to_all x1, waiting for transfers between devices, body(): lax.all_to_all(result, 'region', split_axis=0, concat_axis=1, tiled=True)  10.3 us
    all_to_all x1, starting transfers between devices, body(): lax.all_to_all(result, 'region', split_axis=0, concat_axis=1, tiled=True)  6.4 us
    ppermute x2, starting transfers between devices, from_behind(): return lax.ppermute(block, axis, route)  6 us
    reduce_sum x2, other arithmetic, column_update(): horizontal = jnp.sum(hweight_block[:, :, None] * picked, axis=0)  5.2 us
    gather x4, local copies, waits for them, and re-layouts, pack_blocks(): picked = jnp.take(block_table, safe_list, axis=0)  4.4 us
  transfers between devices with their start and end apart: 7, of which 4 were waited for; matrix products, arithmetic and copies ran while one was open for 7% of the time, Pallas kernels for 0%

commit v1 on v0

--- a/solution.py
+++ b/solution.py
@@ -62,6 +62,18 @@
 
 
 def body(fields, send_list, departure, hweight, base_level, vweight, vertical_op):
+
+    def things_take(original):
+        return jnp.concatenate(
+            jax.lax.all_to_all(
+                jnp.stack(jnp.split(original, jax.lax.axis_size("region"), axis=0), axis=0),
+                axis_name="region",
+                split_axis=0,
+                concat_axis=0,
+            ),
+            axis=1,
+        )
+
     point_total, width_all = fields.shape
     levels = vertical_op.shape[0]
     block_table = fields.reshape(point_total // BLK, BLK, width_all)
@@ -91,7 +103,7 @@
     result = lax.fori_loop(
         0, point_total // step_points, one_step, jnp.zeros((width_all, point_total), jnp.float32)
     )
-    shard_rows = lax.all_to_all(result, "region", split_axis=0, concat_axis=1, tiled=True)
+    shard_rows = things_take(result)
     row_count = width_all // region_count
     padded = padded_2(shard_rows, (("region", 0),), 2)
     global_rows = region_id * row_count + jnp.arange(row_count, dtype=jnp.int32)

time: 179 us -> 191 us (1.067)
  local copies, waits for them, and re-layouts: 39.3 us -> 51 us
    unnamed x9 -> x16, local copies, waits for them, and re-layouts: 3.31 us -> 13.5 us
where the time goes in v1:
time: 191 us; the launch traced here: 190 us
  matrix products  80.4 us (42%)
  local copies, waits for them, and re-layouts  51 us (27%)
  waiting for transfers between devices  24.1 us (13%)
  starting transfers between devices  20.1 us (11%)
  other arithmetic  13.8 us (7%)
    dot_general x2, matrix products, column_update(): jnp.einsum('klp,flp->fkp', level_weights, stacked, precision=exact_mode)  80.4 us
    gather x2, local copies, waits for them, and re-layouts, column_update(): jnp.take(extended, depart_block.reshape(-1), axis=0)  17.8 us
    unnamed x16, local copies, waits for them, and re-layouts  13.5 us
    ppermute x2, waiting for transfers between devices, from_behind(): return lax.ppermute(block, axis, route)  13 us
    all_to_all x1, waiting for transfers between devices, things_take(): jax.lax.all_to_all(jnp.stack(jnp.split(original, jax.lax.axis_size('regio...  10.3 us
    all_to_all x1, starting transfers between devices, things_take(): jax.lax.all_to_all(jnp.stack(jnp.split(original, jax.lax.axis_size('regio...  6.4 us
    ppermute x2, starting transfers between devices, from_behind(): return lax.ppermute(block, axis, route)  6 us
    reduce_sum x2, other arithmetic, column_update(): horizontal = jnp.sum(hweight_block[:, :, None] * picked, axis=0)  5.2 us
  transfers between devices with their start and end apart: 7, of which 4 were waited for; matrix products, arithmetic and copies ran while one was open for 7% of the time, Pallas kernels for 0%

profile of v1, /device:TPU:1, one launch (start us, length us, event | category | flops | bytes accessed | tf_op | source)
XLA Modules:
  0.0 189.8 jit_solution(16045560498128963384)
XLA Ops:
  0.0 1.0 maximum_reduce_fusion
  1.0 1.0 compare_reduce_fusion
  2.0 1.6 gather_fusion.6
  3.6 0.9 select_select_fusion.3
  4.6 4.7 %collective-permute-start = (f32[256,512]{1,0:T(8,128)}, f32[256,512]{1,0:T(8,128)}, u32[]{:S(2)}, u32[]{:S(2)}) collective-permute-start(f32[256,512]{1,0:T(8,128)} %bitcast.11), channel_id=1, source_target_pairs={{0,8},{8,16},{16,24},{1,9},{9,17},{17,25},{2,10},{10,18},{18,26},{... | collective-permute-start | bytes 1572872 | tf_op jit(solution)/shard_map/ppermute | solution.py:13
  9.3 1.6 gather_fusion.7
  10.9 0.9 select_select_fusion.2
  11.9 1.3 collective-permute-start.1
  13.2 0.6 gather_fusion.8
  13.8 0.9 select_select_fusion.1
  14.8 2.1 %collective-permute-start.2 = (f32[256,512]{1,0:T(8,128)}, f32[256,512]{1,0:T(8,128)}, u32[]{:S(2)}, u32[]{:S(2)}) collective-permute-start(f32[256,512]{1,0:T(8,128)} %bitcast.13), channel_id=1, source_target_pairs={{7,0},{0,1},{1,2},{2,3},{3,4},{4,5},{5,6},{6,7},{15,8},{8,9},{9,10... | collective-permute-start | bytes 1572872 | tf_op jit(solution)/shard_map/ppermute | solution.py:19
  16.9 0.6 gather_fusion.9
  17.5 0.9 select_select_fusion
  18.5 0.9 collective-permute-done
  19.4 1.1 constant_dynamic-update-slice_fusion.4
  20.5 12.1 %collective-permute-done.1 = f32[256,512]{1,0:T(8,128)} collective-permute-done((f32[256,512]{1,0:T(8,128)}, f32[256,512]{1,0:T(8,128)}, u32[]{:S(2)}, u32[]{:S(2)}) %collective-permute-start.1) | collective-permute-done | bytes 524320 | tf_op jit(solution)/shard_map/ppermute | solution.py:13
  32.6 1.1 constant_dynamic-update-slice_fusion.3
  33.7 1.1 constant_dynamic-update-slice_fusion.2
  34.8 1.1 constant_dynamic-update-slice_fusion.1
  35.9 0.8 broadcast_in_dim.186.clone
  36.7 112.9 %while.13 = (s32[]{:T(128)}, f32[512,256]{1,0:T(8,128)}, f32[16,256]{1,0:T(8,128)}, s32[16,256]{1,0:T(8,128)}, f32[1280,512]{1,0:T(8,128)S(1)}, /*index=5*/s32[1...) while((s32[]{:T(128)}, f32[512,256]{1,0:T(8,128)}, ...), condition=%wide.region_2.4_spmd, body=%wide.region_0.3_spmd.sunk | while | flops 126881800 | bytes 17125624 | solution.py:103
  36.7 0.7 compare_and_fusion.6
  37.4 8.9 %gather_fusion = f32[2048,512]{1,0:T(8,128)} fusion(f32[1280,512]{1,0:T(8,128)S(1)} %get-tuple-element.297, s32[2048]{0:T(1024)S(1)} %broadcast_clamp_fusion.2), kind=kCustom, calls=%fused_computation.1.clone.1 | custom fusion | bytes 8396800 | tf_op jit(solution)/shard_map/while/body/eval_jaxpr/jit(_take)/gather | solution.py:48
  46.3 0.7 constant_dynamic-slice_fusion.15
  47.0 2.6 %multiply_reduce_fusion.2 = f32[128,512]{1,0:T(8,128)S(1)} fusion(f32[16,128,512]{2,1,0:T(8,128)} %bitcast.74, f32[16,128]{1,0:T(8,128)S(1)} %constant_dynamic-slice_fusion.15, pred[16,128]{1,0:T(8,128)(4,1)S(1)} %get-tuple-element.257), kind=kLoop, calls=%fused_computation.31.clone.1 | loop fusion | flops 3080192 | bytes 4466688 | tf_op jit(solution)/shard_map/while/body/eval_jaxpr/reduce_sum | solution.py:51
  49.7 1.0 constant_dynamic-slice_fusion.16
  50.8 0.1 copy.57
  50.9 0.1 copy.58
  51.0 0.1 copy.59
  51.1 0.9 constant_dynamic-slice_fusion.17
  52.1 40.2 %fusion.62 = f32[4,128,128]{1,0,2:T(4,128)S(1)} fusion(f32[4,128,128]{1,0,2:T(4,128)S(1)} %reshape.418, f32[128,128]{0,1:T(8,128)S(1)} %bitcast.85, s32[128,128]{0,1:T(8,128)S(1)} %get-tuple-element.259, f32[128,128]{0,1:T(8,128)S(1)} %bitcast.86, s32[128,128]{0,1:T(8,128)S(1)} %get-tuple-element.261, f32[128,128]{0,1:T(8,128)S(1)} %bitcast.87, ...), kind=kOutput, calls=%fused_computation.32.clone.2 | convolution fusion | flops 123731968 | bytes 1048576 | tf_op jit(solution)/shard_map/while/body/eval_jaxpr/klp,flp->fkp/dot_general | solution.py:60
  92.2 0.1 copy.60
  92.4 0.7 constant_dynamic-update-slice_fusion.9
  93.1 0.7 compare_and_fusion.6
  93.9 8.9 %gather_fusion = f32[2048,512]{1,0:T(8,128)} fusion(f32[1280,512]{1,0:T(8,128)S(1)} %get-tuple-element.297, s32[2048]{0:T(1024)S(1)} %broadcast_clamp_fusion.2), kind=kCustom, calls=%fused_computation.1.clone.1 | custom fusion | bytes 8396800 | tf_op jit(solution)/shard_map/while/body/eval_jaxpr/jit(_take)/gather | solution.py:48
  102.8 0.7 constant_dynamic-slice_fusion.15
  103.5 2.6 %multiply_reduce_fusion.2 = f32[128,512]{1,0:T(8,128)S(1)} fusion(f32[16,128,512]{2,1,0:T(8,128)} %bitcast.74, f32[16,128]{1,0:T(8,128)S(1)} %constant_dynamic-slice_fusion.15, pred[16,128]{1,0:T(8,128)(4,1)S(1)} %get-tuple-element.257), kind=kLoop, calls=%fused_computation.31.clone.1 | loop fusion | flops 3080192 | bytes 4466688 | tf_op jit(solution)/shard_map/while/body/eval_jaxpr/reduce_sum | solution.py:51
  106.2 1.0 constant_dynamic-slice_fusion.16
  107.2 0.1 copy.57
  107.3 0.1 copy.58
  107.4 0.1 copy.59
  107.5 0.9 constant_dynamic-slice_fusion.17
  108.5 40.2 %fusion.62 = f32[4,128,128]{1,0,2:T(4,128)S(1)} fusion(f32[4,128,128]{1,0,2:T(4,128)S(1)} %reshape.418, f32[128,128]{0,1:T(8,128)S(1)} %bitcast.85, s32[128,128]{0,1:T(8,128)S(1)} %get-tuple-element.259, f32[128,128]{0,1:T(8,128)S(1)} %bitcast.86, s32[128,128]{0,1:T(8,128)S(1)} %get-tuple-element.261, f32[128,128]{0,1:T(8,128)S(1)} %bitcast.87, ...), kind=kOutput, calls=%fused_computation.32.clone.2 | convolution fusion | flops 123731968 | bytes 1048576 | tf_op jit(solution)/shard_map/while/body/eval_jaxpr/klp,flp->fkp/dot_general | solution.py:60
  148.7 0.1 copy.60
  148.9 0.7 constant_dynamic-update-slice_fusion.9
  149.6 1.5 bitcast_dynamic-update-slice_fusion.7
  151.0 1.5 bitcast_dynamic-update-slice_fusion.6
  152.5 1.5 bitcast_dynamic-update-slice_fusion.5
  154.0 1.5 bitcast_dynamic-update-slice_fusion.4
  155.4 1.5 bitcast_dynamic-update-slice_fusion.3
  156.9 1.5 bitcast_dynamic-update-slice_fusion.2
  158.4 1.5 bitcast_dynamic-update-slice_fusion.1
  159.8 1.5 bitcast_dynamic-update-slice_fusion
  161.3 6.4 %all-to-all-start = ((f32[8,64,256]{2,1,0:T(8,128)}), f32[8,64,256]{2,1,0:T(8,128)S(1)}, u32[]{:S(2)}, u32[]{:S(2)}) async-start(f32[8,64,256]{2,1,0:T(8,128)} %bitcast_dynamic-update-slice_fusion), calls=%async_computation | async-start | bytes 1048576 | tf_op jit(solution)/shard_map/all_to_all | solution.py:68
  167.7 0.8 gather_fusion.4
  168.5 0.8 gather_fusion.5
  169.3 0.8 gather_fusion.2
  170.1 0.8 gather_fusion.3
  170.9 0.8 gather_fusion.1
  171.8 10.3 %all-to-all-done = f32[8,64,256]{2,1,0:T(8,128)S(1)} async-done(((f32[8,64,256]{2,1,0:T(8,128)}), f32[8,64,256]{2,1,0:T(8,128)S(1)}, u32[]{:S(2)}, u32[]{:S(2)}) %all-to-all-start) | async-done | bytes 524320 | tf_op jit(solution)/shard_map/all_to_all | solution.py:68
  182.1 2.9 %collective-permute-start.5 = (f32[2,2048]{1,0:T(2,128)S(1)}, f32[2,2048]{1,0:T(2,128)S(1)}, u32[]{:S(2)}, u32[]{:S(2)}) collective-permute-start(f32[2,2048]{1,0:T(2,128)S(1)} %bitcast.92), channel_id=1, source_target_pairs={{1,0},{2,1},{3,2},{4,3},{5,4},{6,5},{7,6},{9,8},{10,9},{11,10},{12... | collective-permute-start | bytes 49160 | tf_op jit(solution)/shard_map/ppermute | solution.py:30
  185.0 2.7 %collective-permute-start.4 = (f32[2,2048]{1,0:T(2,128)S(1)}, f32[2,2048]{1,0:T(2,128)S(1)}, u32[]{:S(2)}, u32[]{:S(2)}) collective-permute-start(f32[2,2048]{1,0:T(2,128)S(1)} %bitcast.91), channel_id=1, source_target_pairs={{0,1},{1,2},{2,3},{3,4},{4,5},{5,6},{6,7},{8,9},{9,10},{10,11},{11... | collective-permute-start | bytes 49160 | tf_op jit(solution)/shard_map/ppermute | solution.py:29
  187.8 0.8 collective-permute-done.4
  188.6 1.2 fusion.26
  (41 shorter events, 0.9 us)
Async XLA Ops:
  0.0 167.7 %copy-start = (f32[128,128]{1,0:T(8,128)S(1)}, f32[128,128]{1,0:T(8,128)}, u32[]{:S(2)}) copy-start(f32[128,128]{1,0:T(8,128)} %param.17) | copy-start | bytes 196612
  0.0 13.2 %copy-start.1 = (f32[256,512]{1,0:T(8,128)S(1)}, f32[256,512]{1,0:T(8,128)}, u32[]{:S(2)}) copy-start(f32[256,512]{1,0:T(8,128)} %param.11) | copy-start | bytes 1572868
  4.6 14.8 %collective-permute-start = (f32[256,512]{1,0:T(8,128)}, f32[256,512]{1,0:T(8,128)}, u32[]{:S(2)}, u32[]{:S(2)}) collective-permute-start(f32[256,512]{1,0:T(8,128)} %bitcast.11), channel_id=1, source_target_pairs={{0,8},{8,16},{16,24},{1,9},{9,17},{17,25},{2,10},{10,18},{18,26},{... | collective-permute-start | bytes 1572872 | tf_op jit(solution)/shard_map/ppermute | solution.py:13
  11.9 20.7 %collective-permute-start.1 = (f32[256,512]{1,0:T(8,128)}, f32[256,512]{1,0:T(8,128)}, u32[]{:S(2)}, u32[]{:S(2)}) collective-permute-start(f32[256,512]{1,0:T(8,128)} %bitcast.12), channel_id=1, source_target_pairs={{8,0},{16,8},{24,16},{9,1},{17,9},{25,17},{10,2},{18,10},{26,18},{... | collective-permute-start | bytes 1572872 | tf_op jit(solution)/shard_map/ppermute | solution.py:13
  14.8 18.9 %collective-permute-start.2 = (f32[256,512]{1,0:T(8,128)}, f32[256,512]{1,0:T(8,128)}, u32[]{:S(2)}, u32[]{:S(2)}) collective-permute-start(f32[256,512]{1,0:T(8,128)} %bitcast.13), channel_id=1, source_target_pairs={{7,0},{0,1},{1,2},{2,3},{3,4},{4,5},{5,6},{6,7},{15,8},{8,9},{9,10... | collective-permute-start | bytes 1572872 | tf_op jit(solution)/shard_map/ppermute | solution.py:19
  18.4 16.3 %collective-permute-start.3 = (f32[256,512]{1,0:T(8,128)}, f32[256,512]{1,0:T(8,128)}, u32[]{:S(2)}, u32[]{:S(2)}) collective-permute-start(f32[256,512]{1,0:T(8,128)} %bitcast.14), channel_id=1, source_target_pairs={{1,0},{2,1},{3,2},{4,3},{5,4},{6,5},{7,6},{0,7},{9,8},{10,9},{11,1... | collective-permute-start | bytes 1572872 | tf_op jit(solution)/shard_map/ppermute | solution.py:19
  161.3 20.8 %all-to-all-start = ((f32[8,64,256]{2,1,0:T(8,128)}), f32[8,64,256]{2,1,0:T(8,128)S(1)}, u32[]{:S(2)}, u32[]{:S(2)}) async-start(f32[8,64,256]{2,1,0:T(8,128)} %bitcast_dynamic-update-slice_fusion), calls=%async_computation | async-start | bytes 1048576 | tf_op jit(solution)/shard_map/all_to_all | solution.py:68
  182.1 5.6 %collective-permute-start.5 = (f32[2,2048]{1,0:T(2,128)S(1)}, f32[2,2048]{1,0:T(2,128)S(1)}, u32[]{:S(2)}, u32[]{:S(2)}) collective-permute-start(f32[2,2048]{1,0:T(2,128)S(1)} %bitcast.92), channel_id=1, source_target_pairs={{1,0},{2,1},{3,2},{4,3},{5,4},{6,5},{7,6},{9,8},{10,9},{11,10},{12... | collective-permute-start | bytes 49160 | tf_op jit(solution)/shard_map/ppermute | solution.py:30
  185.0 3.5 %collective-permute-start.4 = (f32[2,2048]{1,0:T(2,128)S(1)}, f32[2,2048]{1,0:T(2,128)S(1)}, u32[]{:S(2)}, u32[]{:S(2)}) collective-permute-start(f32[2,2048]{1,0:T(2,128)S(1)} %bitcast.91), channel_id=1, source_target_pairs={{0,1},{1,2},{2,3},{3,4},{4,5},{5,6},{6,7},{8,9},{9,10},{10,11},{11... | collective-permute-start | bytes 49160 | tf_op jit(solution)/shard_map/ppermute | solution.py:29
